TPU v7x, 256 devices: a whole 4x4x8 slice. The times are simulated.
256 devices in a mesh: gx: 16 (over x, z_hi), gy: 4 (over y), gz: 4 (over z_lo, core).
Axes of the slice: x: 4, y: 4, z: 8 (z_hi: 4, z_lo: 2; z = z_hi * 2 + z_lo), core: 2. Of those that a mesh axis runs over, the one named last changes fastest.
Arguments:
- flow_field: bfloat16 [512, 256, 2048], P('gx', 'gy', 'gz'), may hold values from -96 to 96
- left_x: bfloat16 [512, 128], P('gx'), may hold values from -0.0234375 to 0.0234375
- last_x: bfloat16 [512, 128], P('gx'), may hold values from -0.25 to 0.25
- last_y: bfloat16 [256, 128], P('gy'), may hold values from -0.005859375 to 0.005859375
- right_y: bfloat16 [256, 256], P('gy'), may hold values from -0.375 to 0.375
- right_m: bfloat16 [2048, 256], P('gz'), may hold values from -0.125 to 0.125
- last_m: bfloat16 [2048, 256], P('gz'), may hold values from -0.125 to 0.125
Outputs:
- core_first: float32 [512, 128], P('gx')
- core_middle: float32 [128, 256, 128], P(('gx', 'gz'), 'gy')
- core_last: float32 [128, 2048], P(None, 'gz')
All inputs are finite; a program needn't handle non-finite values.
Results may differ from a plain program's by a relative error of at most 0.0053.
Values sent between devices are 32-bit elements; how exact they have to be, the bound alone decides.
A program may use at most 64 MiB of HBM per device.

v0:
```python
import jax
import jax.numpy as jnp
from jax import lax
from jax.sharding import PartitionSpec as P


def normal_solve(system, right_side):
    gram_matrix = jnp.dot(system, system.T, precision=lax.Precision.HIGHEST)
    factor = jnp.linalg.cholesky(gram_matrix)
    return jax.scipy.linalg.cho_solve((factor, True), right_side)


def per_device(flow_field, left_x, last_x, last_y, right_y, right_m, last_m):
    highest = lax.Precision.HIGHEST
    x_cells, y_cells, m_cells = flow_field.shape
    rank_cols = left_x.shape[1]
    sketch_cols = right_m.shape[1]
    flat_field = flow_field.reshape(x_cells * y_cells, m_cells)
    first_terms = jnp.dot(flat_field, right_m, preferred_element_type=jnp.float32).reshape(
        x_cells, y_cells, sketch_cols
    )
    first_part = jnp.sum(first_terms * right_y.astype(jnp.float32)[None], axis=1)
    first_rows = lax.psum(first_part, ("gy", "gz"))
    left_wide = left_x.astype(jnp.float32)
    first_gram = lax.psum(jnp.dot(left_wide.T, first_rows, precision=highest), "gx")
    core_first = normal_solve(first_gram, jnp.dot(first_gram, first_rows.T, precision=highest)).T
    khatri = (last_x.astype(jnp.float32)[:, None, :] * last_y.astype(jnp.float32)[None]).astype(
        jnp.bfloat16
    )
    khatri = khatri.reshape(x_cells * y_cells, rank_cols)
    last_part = jnp.dot(khatri.T, flat_field, preferred_element_type=jnp.float32)
    core_last = lax.psum(last_part, ("gx", "gy"))
    last_gram = lax.psum(jnp.dot(core_last, last_m.astype(jnp.float32), precision=highest), "gz")
    pinv_last = normal_solve(last_gram, last_gram).T
    flat_terms = jnp.dot(flat_field, last_m, preferred_element_type=jnp.float32)
    last_terms = flat_terms.reshape(x_cells, y_cells * sketch_cols)
    row_share = rank_cols // lax.axis_size(("gx", "gz"))
    middle_sums = lax.psum_scatter(
        jnp.dot(left_wide.T, last_terms, precision=highest).reshape(
            row_share * lax.axis_size(("gx", "gz")), y_cells, sketch_cols
        ),
        ("gx", "gz"),
        scatter_dimension=0,
        tiled=True,
    )
    core_middle = jnp.dot(
        middle_sums.reshape(row_share * y_cells, sketch_cols), pinv_last, precision=highest
    )
    core_middle = core_middle.reshape(row_share, y_cells, rank_cols)
    return (core_first, core_middle, core_last)


def solution(mesh):
    return jax.shard_map(
        per_device,
        mesh=mesh,
        in_specs=(
            P("gx", "gy", "gz"),
            P("gx", None),
            P("gx", None),
            P("gy", None),
            P("gy", None),
            P("gz", None),
            P("gz", None),
        ),
        out_specs=(P("gx", None), P(("gx", "gz"), "gy", None), P(None, "gz")),
        check_vma=False,
    )
```

profile of v0, /device:TPU:1, one launch (start us, length us, event | category | flops | bytes accessed | tf_op | source)
XLA Modules:
  0.0 930.0 jit_solution(4668367135638992668)
XLA Ops:
  8.0 0.0 copy-start
  8.0 0.0 copy-start.4
  8.0 0.0 copy-start.5
  8.0 0.0 all-reduce.6.cloned.1.call-start
  8.1 0.9 convert_element_type.16
  9.0 0.7 convert_element_type.15
  9.7 0.0 copy-done
  9.7 1.2 convolution_bitcast_fusion
  10.8 0.0 all-reduce.6.cloned.1.call-update
  10.9 0.0 all-reduce.4.cloned.1.call-start
  10.9 0.0 copy-done.4
  10.9 0.0 copy-done.5
  10.9 0.0 copy-start.3
  11.0 0.0 copy-start.2
  11.0 0.7 multiply_reduce_fusion
  11.7 54.8 %psum.28 = f32[32,256]{1,0:T(8,128)S(1)} all-reduce(f32[32,256]{1,0:T(8,128)S(1)} %multiply_reduce_fusion), channel_id=1, replica_groups=mesh['gx'=16,'gy'=4,'gz'=4] {'gy','gz'}, use_global_device_ids=true, to_apply=%region_1.0 | all-reduce | flops 8192 | bytes 65536 | tf_op jit(solution)/shard_map/psum | solution.py:23
  66.5 0.0 copy-done.3
  66.5 0.9 convolution_bitcast_fusion.2
  67.5 0.0 all-reduce.4.cloned.1.call-update
  67.5 0.0 all-reduce.8.cloned.1.call-start
  67.5 0.0 copy-done.2
  67.5 2.0 fusion.16
  69.5 2.8 reshape.46
  72.3 589.0 %all-reduce.6.cloned.1.call-done = f32[128,512]{1,0:T(8,128)} async-done(((f32[128,512]{1,0:T(8,128)}), f32[128,512]{1,0:T(8,128)}) %all-reduce.6.cloned.1.call-update) | async-done | bytes 262160 | tf_op jit(solution)/shard_map/psum | solution.py:32
  661.3 1.9 fusion.18
  663.2 0.0 all-reduce.8.cloned.1.call-update
  663.3 0.0 reduce-scatter.2.cloned.1.call-start
  663.3 10.1 %fusion.17 = f32[16384,128]{1,0:T(8,128)} fusion(f32[32,16384]{1,0:T(8,128)} %reshape.46, bf16[32,128]{1,0:T(8,128)(2,1)S(1)} %copy-done.3), kind=kOutput, calls=%fused_computation.32 | convolution fusion | flops 805306368 | bytes 10493952 | tf_op jit(solution)/shard_map/dot_general | solution.py:39
  673.4 9.2 copy.11
  682.6 0.0 reduce-scatter.2.cloned.1.call-update
  682.6 0.0 copy-start.1
  682.6 161.7 %all-reduce.4.cloned.1.call-done = f32[128,256]{0,1:T(8,128)} async-done(((f32[128,256]{0,1:T(8,128)}), f32[128,256]{0,1:T(8,128)}) %all-reduce.4.cloned.1.call-update) | async-done | bytes 131088 | tf_op jit(solution)/shard_map/psum | solution.py:25
  844.3 1.4 fusion.14
  845.6 0.1 copy.10
  845.8 11.7 %cholesky.44 = f32[128,128]{1,0:T(8,128)S(1)} custom-call(f32[128,128]{1,0:T(8,128)S(1)} %fusion.13), custom_call_target="Cholesky" | custom-call | tf_op jit(solution)/shard_map/jit(cholesky)/cholesky | solution.py:9
  857.5 0.6 compare_reduce_fusion.1
  858.1 0.7 fusion.3
  858.8 9.8 %custom-call.16 = f32[1,128,128]{1,2,0:T(8,128)S(1)} custom-call(f32[1,128,128]{2,1,0:T(8,128)S(1)} %fusion.3), custom_call_target="InvertDiagBlocksLowerTriangular" | custom-call | tf_op jit(solution)/shard_map/jit(_cho_solve)/triangular_solve | solution.py:10
  868.6 1.3 fusion.15
  869.9 0.3 fusion.11
  870.2 0.9 fusion.9
  871.1 23.5 %all-reduce.8.cloned.1.call-done = f32[128,256]{1,0:T(8,128)} async-done(((f32[128,256]{1,0:T(8,128)}), f32[128,256]{1,0:T(8,128)}) %all-reduce.8.cloned.1.call-update) | async-done | bytes 131088 | tf_op jit(solution)/shard_map/psum | solution.py:33
  894.5 1.3 fusion.19
  895.8 0.1 copy.12
  895.9 11.7 %cholesky.55 = f32[128,128]{1,0:T(8,128)S(1)} custom-call(f32[128,128]{1,0:T(8,128)S(1)} %fusion.8), custom_call_target="Cholesky" | custom-call | tf_op jit(solution)/shard_map/jit(cholesky)/cholesky | solution.py:9
  907.7 0.6 compare_reduce_fusion
  908.3 0.7 fusion.4
  909.0 9.8 %custom-call.17 = f32[1,128,128]{1,2,0:T(8,128)S(1)} custom-call(f32[1,128,128]{2,1,0:T(8,128)S(1)} %fusion.4), custom_call_target="InvertDiagBlocksLowerTriangular" | custom-call | tf_op jit(solution)/shard_map/jit(_cho_solve)/triangular_solve | solution.py:10
  918.8 1.2 fusion.6
  920.0 0.3 convolution_bitcast_fusion.1
  920.3 0.0 reduce-scatter.2.cloned.1.call-done
  920.3 1.8 fusion.20
  922.1 0.0 copy-done.1
  922.1 0.7 copy.16
  (5 shorter events, 0.1 us)
Async XLA Ops:
  8.0 1.7 copy-start
  8.0 2.9 copy-start.4
  8.0 2.9 copy-start.5
  8.0 653.3 %all-reduce.6.cloned.1.call-start = ((), (), s32[]{:S(2)}) async-start(), calls=%async_computation.3 | async-start | bytes 524288 | tf_op jit(solution)/shard_map/psum | solution.py:32
  10.9 833.4 %all-reduce.4.cloned.1.call-start = ((), (), s32[]{:S(2)}) async-start(), calls=%async_computation.1 | async-start | bytes 262144 | tf_op jit(solution)/shard_map/psum | solution.py:25
  10.9 55.6 %copy-start.3 = (bf16[32,128]{1,0:T(8,128)(2,1)S(1)}, bf16[32,128]{1,0:T(8,128)(2,1)}, u32[]{:S(2)}) copy-start(bf16[32,128]{1,0:T(8,128)(2,1)} %param.9) | copy-start | bytes 24580
  11.0 56.6 %copy-start.2 = (bf16[512,256]{1,0:T(8,128)(2,1)S(1)}, bf16[512,256]{1,0:T(8,128)(2,1)}, u32[]{:S(2)}) copy-start(bf16[512,256]{1,0:T(8,128)(2,1)} %param.14) | copy-start | bytes 786436
  67.5 827.1 %all-reduce.8.cloned.1.call-start = ((), (), s32[]{:S(2)}) async-start(), calls=%async_computation.4 | async-start | bytes 262144 | tf_op jit(solution)/shard_map/psum | solution.py:33
  663.3 257.1 %reduce-scatter.2.cloned.1.call-start = ((), (), s32[]{:S(2)}) async-start(), calls=%async_computation.2 | async-start | bytes 8519680 | tf_op jit(solution)/shard_map/reduce_scatter | solution.py:38
  682.6 239.5 %copy-start.1 = (f32[128,512]{1,0:T(8,128)S(1)}, f32[128,512]{1,0:T(8,128)}, u32[]{:S(2)}) copy-start(f32[128,512]{1,0:T(8,128)} %all-reduce.6.cloned.1.call-done) | copy-start | bytes 786436
Sparse Core Ops, SparseCore 0:
  12.1 649.2 all-reduce.5
  664.1 180.0 all-reduce.3
  847.7 46.8 all-reduce.7
Sparse Core Ops, SparseCore 1:
  682.7 170.6 reduce-scatter.1
where the time goes:
time: 930 us
  waiting for transfers between devices  774 us (83%)
  blocking collectives  54.8 us (6%)
  other arithmetic  47.3 us (5%)
  matrix products  25.1 us (3%)
  between operations  15.4 us (2%)
  local copies, waits for them, and re-layouts  12.9 us (1%)
    psum x1, waiting for transfers between devices, per_device(): core_last = lax.psum(last_part, ('gx', 'gy'))  589 us
    psum x1, waiting for transfers between devices, per_device(): lax.psum(jnp.dot(left_wide.T, first_rows, precision=highest), 'gx')  162 us
    psum x1, blocking collectives, per_device(): first_rows = lax.psum(first_part, ('gy', 'gz'))  54.8 us
    another operation x6, other arithmetic, normal_solve(): factor = jnp.linalg.cholesky(gram_matrix)  24.8 us
    psum x1, waiting for transfers between devices, per_device(): lax.psum(jnp.dot(core_last, last_m.astype(jnp.float32), precision=highest...  23.5 us
    another operation x4, other arithmetic, normal_solve(): return jax.scipy.linalg.cho_solve((factor, True), right_side)  20.9 us
  transfers between devices with their start and end apart: 4, of which 3 were waited for; matrix products, arithmetic and copies ran while one was open for 9% of the time, Pallas kernels for 0%

commit v1 on v0

--- a/solution.py
+++ b/solution.py
@@ -29,7 +29,8 @@
     )
     khatri = khatri.reshape(x_cells * y_cells, rank_cols)
     last_part = jnp.dot(khatri.T, flat_field, preferred_element_type=jnp.float32)
-    core_last = lax.psum(last_part, ("gx", "gy"))
+    inner = lax.psum(last_part, "gx")
+    core_last = lax.psum(inner, "gy")
     last_gram = lax.psum(jnp.dot(core_last, last_m.astype(jnp.float32), precision=highest), "gz")
     pinv_last = normal_solve(last_gram, last_gram).T
     flat_terms = jnp.dot(flat_field, last_m, preferred_element_type=jnp.float32)

time: 930 us -> 467 us (0.50)
  waiting for transfers between devices: 774 us -> 308 us
    psum x1, waiting for transfers between devices: 589 us -> 49.9 us  [per_device(): core_last = lax.psum(inner, 'gy')]
    reduce_scatter x1, waiting for transfers between devices: 0.03 us -> 98.3 us  [per_device(): lax.psum_scatter(jnp.dot(left_wide.T, last_terms, precision=highest).resh...]
    psum x1, waiting for transfers between devices: 23.5 us -> 0.01 us  [per_device(): lax.psum(jnp.dot(core_last, last_m.astype(jnp.float32), precision=highest...]
  transfers between devices with their start and end apart: 4 -> 4, of which waited for: 3 -> 3; matrix products, arithmetic and copies ran while one was open for 9% -> 16% of each run, Pallas kernels for 0% -> 0%
where the time goes in v1:
time: 467 us; the launch traced here: 463 us
  waiting for transfers between devices  308 us (66%)
  blocking collectives  53.8 us (12%)
  other arithmetic  46.6 us (10%)
  matrix products  24.2 us (5%)
  between operations  15.4 us (3%)
  local copies, waits for them, and re-layouts  14.4 us (3%)
    psum x1, waiting for transfers between devices, per_device(): lax.psum(jnp.dot(left_wide.T, first_rows, precision=highest), 'gx')  160 us
    reduce_scatter x1, waiting for transfers between devices, per_device(): lax.psum_scatter(jnp.dot(left_wide.T, last_terms, precision=highest).resh...  98.3 us
    psum x1, blocking collectives, per_device(): first_rows = lax.psum(first_part, ('gy', 'gz'))  53.8 us
    psum x1, waiting for transfers between devices, per_device(): core_last = lax.psum(inner, 'gy')  49.9 us
    another operation x6, other arithmetic, normal_solve(): factor = jnp.linalg.cholesky(gram_matrix)  24.8 us
    another operation x4, other arithmetic, normal_solve(): return jax.scipy.linalg.cho_solve((factor, True), right_side)  20.9 us
    dot_general x1, matrix products, per_device(): jnp.dot(left_wide.T, last_terms, precision=highest)  10.1 us
  transfers between devices with their start and end apart: 4, of which 3 were waited for; matrix products, arithmetic and copies ran while one was open for 16% of the time, Pallas kernels for 0%

profile of v1, /device:TPU:1, one launch (start us, length us, event | category | flops | bytes accessed | tf_op | source)
XLA Modules:
  0.0 462.7 jit_solution(9126587958095260097)
XLA Ops:
  8.0 0.0 copy-start
  8.0 0.0 all-reduce.9.cloned.1.call-start
  8.1 0.9 convert_element_type.14
  9.0 0.6 copy-done
  9.6 0.0 copy-start.5
  9.6 0.0 copy-start.6
  9.6 0.0 copy-start.4
  9.6 1.7 multiply_reduce_fusion
  11.3 0.0 copy-start.3
  11.3 53.8 %psum.35 = f32[32,256]{1,0:T(8,128)S(1)} all-reduce(f32[32,256]{1,0:T(8,128)S(1)} %multiply_reduce_fusion), channel_id=1, replica_groups=mesh['gx'=16,'gy'=4,'gz'=4] {'gy','gz'}, use_global_device_ids=true, to_apply=%region_1.0 | all-reduce | flops 8192 | bytes 65536 | tf_op jit(solution)/shard_map/psum | solution.py:23
  65.2 0.0 copy-done.5
  65.2 0.0 copy-done.6
  65.2 0.0 copy-done.4
  65.2 0.9 convolution_bitcast_fusion.2
  66.1 1.2 convolution_bitcast_fusion
  67.3 0.0 all-reduce.9.cloned.1.call-update
  67.3 0.0 all-reduce.5.cloned.1.call-start
  67.4 159.9 %all-reduce.9.cloned.1.call-done = (f32[128,256]{0,1:T(8,128)}, f32[128,512]{1,0:T(8,128)}) async-done(((f32[128,256]{0,1:T(8,128)}, f32[128,512]{1,0:T(8,128)}), (f32[128,256]{0,1:T(8,128)}, f32[128,512]{1,0:T(8,128)})) %all-reduce.9.cloned.1.call-update) | async-done | bytes 393232 | tf_op jit(solution)/shard_map/psum | solution.py:25
  227.2 0.0 all-reduce.5.cloned.1.call-update
  227.3 0.0 all-reduce.7.cloned.1.call-start
  227.3 0.0 copy-done.3
  227.3 2.0 fusion.16
  229.3 2.8 reshape.46
  232.1 49.9 %all-reduce.5.cloned.1.call-done = f32[128,512]{1,0:T(8,128)} async-done(((f32[128,512]{1,0:T(8,128)}), f32[128,512]{1,0:T(8,128)}) %all-reduce.5.cloned.1.call-update) | async-done | bytes 262160 | tf_op jit(solution)/shard_map/psum | solution.py:33
  282.0 1.9 fusion.18
  283.9 0.0 all-reduce.7.cloned.1.call-update
  283.9 0.0 reduce-scatter.2.cloned.1.call-start
  283.9 10.1 %fusion.17 = f32[16384,128]{1,0:T(8,128)} fusion(f32[32,16384]{1,0:T(8,128)} %reshape.46, bf16[32,128]{1,0:T(8,128)(2,1)S(1)} %copy-done.4), kind=kOutput, calls=%fused_computation.32 | convolution fusion | flops 805306368 | bytes 10493952 | tf_op jit(solution)/shard_map/dot_general | solution.py:40
  294.0 9.2 %copy.11 = f32[128,64,256]{2,1,0:T(8,128)} copy(f32[128,64,256]{0,2,1:T(8,128)} %bitcast.58) | data formatting | bytes 16777216 | tf_op jit(solution)/shard_map/reshape | solution.py:40
  303.2 0.0 copy-start.1
  303.2 0.0 reduce-scatter.2.cloned.1.call-update
  303.2 0.0 copy-start.2
  303.2 0.9 copy-done.1
  304.1 0.4 fusion.14
  304.5 0.1 copy.10
  304.6 11.7 %cholesky.44 = f32[128,128]{1,0:T(8,128)S(1)} custom-call(f32[128,128]{1,0:T(8,128)S(1)} %fusion.13), custom_call_target="Cholesky" | custom-call | tf_op jit(solution)/shard_map/jit(cholesky)/cholesky | solution.py:9
  316.4 0.6 compare_reduce_fusion.1
  317.0 0.7 fusion.3
  317.7 9.8 %custom-call.16 = f32[1,128,128]{1,2,0:T(8,128)S(1)} custom-call(f32[1,128,128]{2,1,0:T(8,128)S(1)} %fusion.3), custom_call_target="InvertDiagBlocksLowerTriangular" | custom-call | tf_op jit(solution)/shard_map/jit(_cho_solve)/triangular_solve | solution.py:10
  327.5 0.4 fusion.15
  327.9 0.3 fusion.11
  328.2 0.9 fusion.9
  329.0 0.0 all-reduce.7.cloned.1.call-done
  329.0 1.3 fusion.19
  330.3 0.1 copy.12
  330.4 11.7 %cholesky.55 = f32[128,128]{1,0:T(8,128)S(1)} custom-call(f32[128,128]{1,0:T(8,128)S(1)} %fusion.8), custom_call_target="Cholesky" | custom-call | tf_op jit(solution)/shard_map/jit(cholesky)/cholesky | solution.py:9
  342.2 0.6 compare_reduce_fusion
  342.8 0.7 fusion.4
  343.5 9.8 %custom-call.17 = f32[1,128,128]{1,2,0:T(8,128)S(1)} custom-call(f32[1,128,128]{2,1,0:T(8,128)S(1)} %fusion.4), custom_call_target="InvertDiagBlocksLowerTriangular" | custom-call | tf_op jit(solution)/shard_map/jit(_cho_solve)/triangular_solve | solution.py:10
  353.3 1.2 fusion.6
  354.5 0.3 convolution_bitcast_fusion.1
  354.8 98.3 %reduce-scatter.2.cloned.1.call-done = f32[2,64,256]{2,1,0:T(8,128)} async-done(((f32[128,64,256]{2,1,0:T(8,128)}), f32[2,64,256]{2,1,0:T(8,128)}) %reduce-scatter.2.cloned.1.call-update) | async-done | bytes 131088 | tf_op jit(solution)/shard_map/reduce_scatter | solution.py:39
  453.1 1.8 fusion.20
  454.9 0.0 copy-done.2
  454.9 0.7 copy.17
  (6 shorter events, 0.1 us)
Async XLA Ops:
  8.0 1.6 copy-start
  8.0 219.2 %all-reduce.9.cloned.1.call-start = ((), (), s32[]{:S(2)}) async-start(), calls=%async_computation.4 | async-start | bytes 786432 | tf_op jit(solution)/shard_map/psum | solution.py:25
  9.6 55.6 %copy-start.5 = (bf16[64,128]{1,0:T(8,128)(2,1)S(1)}, bf16[64,128]{1,0:T(8,128)(2,1)}, u32[]{:S(2)}) copy-start(bf16[64,128]{1,0:T(8,128)(2,1)} %param.11) | copy-start | bytes 49156
  9.6 55.6 %copy-start.6 = (bf16[32,128]{1,0:T(8,128)(2,1)S(1)}, bf16[32,128]{1,0:T(8,128)(2,1)}, u32[]{:S(2)}) copy-start(bf16[32,128]{1,0:T(8,128)(2,1)} %param.10) | copy-start | bytes 24580
  9.6 55.6 %copy-start.4 = (bf16[32,128]{1,0:T(8,128)(2,1)S(1)}, bf16[32,128]{1,0:T(8,128)(2,1)}, u32[]{:S(2)}) copy-start(bf16[32,128]{1,0:T(8,128)(2,1)} %param.9) | copy-start | bytes 24580
  11.3 216.0 %copy-start.3 = (bf16[512,256]{1,0:T(8,128)(2,1)S(1)}, bf16[512,256]{1,0:T(8,128)(2,1)}, u32[]{:S(2)}) copy-start(bf16[512,256]{1,0:T(8,128)(2,1)} %param.14) | copy-start | bytes 786436
  67.3 214.7 %all-reduce.5.cloned.1.call-start = ((), (), s32[]{:S(2)}) async-start(), calls=%async_computation.2 | async-start | bytes 524288 | tf_op jit(solution)/shard_map/psum | solution.py:33
  227.3 101.8 %all-reduce.7.cloned.1.call-start = ((), (), s32[]{:S(2)}) async-start(), calls=%async_computation.3 | async-start | bytes 262144 | tf_op jit(solution)/shard_map/psum | solution.py:34
  283.9 169.2 %reduce-scatter.2.cloned.1.call-start = ((), (), s32[]{:S(2)}) async-start(), calls=%async_computation.1 | async-start | bytes 8519680 | tf_op jit(solution)/shard_map/reduce_scatter | solution.py:39
  303.2 0.9 copy-start.1
  303.2 151.6 %copy-start.2 = (f32[128,512]{1,0:T(8,128)S(1)}, f32[128,512]{1,0:T(8,128)}, u32[]{:S(2)}) copy-start(f32[128,512]{1,0:T(8,128)} %all-reduce.5.cloned.1.call-done) | copy-start | bytes 786436
Sparse Core Ops, SparseCore 0:
  67.4 159.7 all-reduce.8
  229.6 52.3 all-reduce.4
  285.4 43.6 all-reduce.6
Sparse Core Ops, SparseCore 1:
  303.3 149.7 reduce-scatter.1
